TPU v7x, 32 devices: a whole 2x2x4 slice. The times are simulated.
32 devices in a mesh: tok: 16 (over z, x, core), lyr: 2 (over y).
Axes of the slice: x: 2, y: 2, z: 4, core: 2. Of those that a mesh axis runs over, the one named last changes fastest.
Arguments:
- feature_codes: bfloat16 [4, 2048, 2, 256], P('lyr', 'tok'), may hold values from 0 to 21, as said below
- block_ids: int32 [4, 2048, 2], P('lyr', 'tok'), may hold values from 0 to 31, all different within a row; in each aligned block of 128 rows (0 to 127, 128 to 255, ..., all dimensions but the last counted through in order) at most 16 rows name the same one
- target_layer: int32 [2048], P('tok'), may hold values from 0 to 3
- request_ids: int32 [2048], P('tok'), may hold values from 0 to 15
- target_resid: bfloat16 [2048, 2304], P('tok'), may hold values from -6 to 6
- decoder: bfloat16 [4, 8192, 2304], P('lyr', 'tok'), may hold values from -0.25 to 0.25
Outputs:
- scores: bfloat16 [4, 2048, 2, 256], P('lyr', 'tok')
- request_totals: float32 [16, 4, 8192], P(None, 'lyr', 'tok')
Inputs may be any that keep to these rules, and one draw needn't show every extreme that they name: `block_ids`: the 2 panel indices of one token at one source layer are distinct; among the 128 tokens of one index of tok at one source layer no panel is named by more than 16 of them, a bound that some block reaches. `feature_codes`: nonnegative, with many entries zero.
All inputs are finite; a program needn't handle non-finite values.
Results may differ from a plain program's by a relative error of at most 0.0053.
Values may be sent and summed in bfloat16 or wider, within the bound.
A program may use at most 64 MiB of HBM per device.

v0:
```python
import jax
import jax.numpy as jnp
from jax import lax
from jax.sharding import PartitionSpec as P

PANELS = 32
REQUESTS = 16
CAP = 16


def slot_of(flat_ids):
    one_hot = (flat_ids[:, None] == jnp.arange(PANELS, dtype=jnp.int32)[None, :]).astype(jnp.int32)
    before = jnp.cumsum(one_hot, axis=0) - one_hot
    return flat_ids * CAP + jnp.sum(before * one_hot, axis=1)


def source_of(slot_ids):
    row_count = slot_ids.shape[0]
    empty = jnp.full((PANELS * CAP,), row_count, jnp.int32)
    return empty.at[slot_ids].set(jnp.arange(row_count, dtype=jnp.int32))


def take_rows(table, index):
    return jnp.take(table, index, axis=0)


def pad_zero(table):
    return jnp.concatenate([table, jnp.zeros((1,) + table.shape[1:], table.dtype)], axis=0)


def normalize_error(resid_rows, rebuilt):
    error = resid_rows.astype(jnp.float32) - rebuilt
    spread = jnp.mean(error * error, axis=-1, keepdims=True)
    return (error * lax.rsqrt(spread + 1e-06)).astype(jnp.bfloat16)


def per_device(feature_codes, block_ids, target_layer, request_ids, target_resid, decoder):
    layers_here, count, kact, panel = feature_codes.shape
    width = target_resid.shape[1]
    tok_count = lax.axis_size("tok")
    per_dev = PANELS // tok_count
    rows_here = count * kact
    first_layer = lax.axis_index("lyr") * layers_here
    layer_ids = first_layer + jnp.arange(layers_here, dtype=jnp.int32)
    alive_mask = (layer_ids[:, None] <= target_layer[None, :]).astype(feature_codes.dtype)
    masked = feature_codes * alive_mask[:, :, None, None]
    flat_ids = block_ids.reshape(layers_here, rows_here)
    slot_ids = jax.vmap(slot_of)(flat_ids)
    source_rows = jax.vmap(source_of)(slot_ids)
    token_of = source_rows // kact
    code_rows = jax.vmap(pad_zero)(masked.reshape(layers_here, rows_here, panel))
    send_codes = jax.vmap(take_rows)(code_rows, source_rows).reshape(
        layers_here, tok_count, per_dev, CAP, panel
    )
    panel_weights = decoder.reshape(layers_here, per_dev, panel, width)
    slot_requests = jnp.take(pad_zero(request_ids), token_of, axis=0).reshape(
        layers_here, tok_count, per_dev, CAP
    )
    received, request_slots = (
        lax.all_to_all(send_codes, "tok", split_axis=1, concat_axis=1, tiled=True),
        lax.all_to_all(slot_requests, "tok", split_axis=1, concat_axis=1, tiled=True),
    )
    built = jnp.einsum(
        "lspcj,lpjd->lspcd", received, panel_weights, preferred_element_type=jnp.float32
    ).astype(jnp.bfloat16)
    returned = lax.all_to_all(built, "tok", split_axis=1, concat_axis=1, tiled=True).reshape(
        layers_here, PANELS * CAP, width
    )
    per_row = jax.vmap(take_rows)(returned, slot_ids)
    partial_value = jnp.sum(
        per_row.astype(jnp.float32).reshape(layers_here, count, kact, width), axis=(0, 2)
    )
    rebuilt = lax.psum(partial_value, "lyr")
    gradient = normalize_error(target_resid, rebuilt)
    send_grad = jnp.take(pad_zero(gradient), token_of, axis=0).reshape(
        layers_here, tok_count, per_dev, CAP, width
    )
    received_grad = lax.all_to_all(send_grad, "tok", split_axis=1, concat_axis=1, tiled=True)
    projected_slots = jnp.einsum(
        "lspcd,lpjd->lspcj", received_grad, panel_weights, preferred_element_type=jnp.float32
    ).astype(jnp.bfloat16)
    coming_back = lax.all_to_all(
        projected_slots, "tok", split_axis=1, concat_axis=1, tiled=True
    ).reshape(layers_here, PANELS * CAP, panel)
    picked = jax.vmap(take_rows)(coming_back, slot_ids).reshape(layers_here, count, kact, panel)
    attribution_rows = masked.astype(jnp.float32) * picked.astype(jnp.float32)
    scores = attribution_rows.astype(jnp.bfloat16)
    attribution = received.astype(jnp.float32) * projected_slots.astype(jnp.float32)
    members = (request_slots[..., None] == jnp.arange(REQUESTS, dtype=jnp.int32)).astype(
        jnp.float32
    )
    owned = jnp.einsum("lspcr,lspcj->rlpj", members, attribution, precision=lax.Precision.HIGHEST)
    request_totals = owned.reshape(REQUESTS, layers_here, per_dev * panel)
    return (scores, request_totals)


def solution(mesh):
    placed = (
        P("lyr", "tok", None, None),
        P("lyr", "tok", None),
        P("tok"),
        P("tok"),
        P("tok", None),
        P("lyr", "tok", None),
    )
    return jax.shard_map(
        per_device,
        mesh=mesh,
        in_specs=placed,
        out_specs=(P("lyr", "tok", None, None), P(None, "lyr", "tok")),
        check_vma=False,
    )
```

profile of v0, /device:TPU:0, one launch (start us, length us, event | category | flops | bytes accessed | tf_op | source)
XLA Modules:
  0.0 417.3 jit_solution(11479595752540939134)
XLA Ops:
  7.2 0.9 copy.84
  9.0 1.2 reduce-window.6
  10.9 24.5 %scatter_fusion = s32[2,512]{1,0:T(2,128)S(1)} fusion(s32[2,512]{1,0:T(2,128)S(1)} %broadcast_in_dim.71, s32[512]{0:T(512)S(1)} %bitcast.74, s32[512]{0:T(512)S(1)} %bitcast.84), kind=kCustom, calls=%fused_computation.5 | custom fusion | bytes 10240 | tf_op jit(solution)/shard_map/vmap()/scatter | solution.py:20
  36.7 5.5 %gather_fusion.2 = bf16[1024,256]{1,0:T(8,128)(2,1)S(1)} fusion(bf16[2,257,256]{2,0,1:T(2,128)(2,1)S(1)} %concatenate.9, s32[1024]{0:T(1024)S(1)} %bitcast.73), kind=kCustom, calls=%fused_computation.2 | custom fusion | bytes 1056768 | tf_op jit(solution)/shard_map/vmap(jit(_take))/gather | solution.py:24
  42.4 21.5 %all_to_all.25 = bf16[2,16,2,16,256]{4,3,2,0,1:T(8,128)(2,1)S(1)} all-to-all(bf16[2,16,2,16,256]{4,3,2,0,1:T(8,128)(2,1)S(1)} %copy.91), channel_id=1, replica_groups=mesh['tok'=16,'lyr'=2] {'tok'}, dimensions={1} | all-to-all | bytes 1048576 | tf_op jit(solution)/shard_map/all_to_all | solution.py:60
  63.9 3.7 fusion
  67.6 2.7 copy.93
  70.3 4.6 %all-to-all-start.1 = ((bf16[2,16,2,16,2304]{4,3,2,0,1:T(8,128)(2,1)}), bf16[2,16,2,16,2304]{4,3,2,0,1:T(8,128)(2,1)}, u32[]{:S(2)}, u32[]{:S(2)}) async-start(bf16[2,16,2,16,2304]{4,3,2,0,1:T(8,128)(2,1)} %copy.93), calls=%async_computation.1 | async-start | bytes 9437184 | tf_op jit(solution)/shard_map/all_to_all | solution.py:66
  75.2 86.4 %all-to-all-done.1 = bf16[2,16,2,16,2304]{4,3,2,0,1:T(8,128)(2,1)} async-done(((bf16[2,16,2,16,2304]{4,3,2,0,1:T(8,128)(2,1)}), bf16[2,16,2,16,2304]{4,3,2,0,1:T(8,128)(2,1)}, u32[]{:S(2)}, u32[]{:S(2)}) %all-to-all-start.1) | async-done | bytes 4718624 | tf_op jit(solution)/shard_map/all_to_all | solution.py:66
  161.5 4.9 %copy.94 = bf16[2,16,2,16,2304]{4,3,2,1,0:T(8,128)(2,1)} copy(bf16[2,16,2,16,2304]{4,3,2,0,1:T(8,128)(2,1)} %all-to-all-done.1) | data formatting | bytes 9437184 | tf_op jit(solution)/shard_map/all_to_all | solution.py:66
  166.4 13.5 %gather_fusion.3 = bf16[512,2304]{1,0:T(8,128)(2,1)} fusion(bf16[2,512,2304]{2,1,0:T(8,128)(2,1)} %bitcast.72, s32[512]{0:T(512)S(1)} %bitcast.70), kind=kCustom, calls=%fused_computation.3 | custom fusion | bytes 4722688 | tf_op jit(solution)/shard_map/vmap(jit(_take))/gather | solution.py:24
  179.9 2.4 convert_reduce_fusion
  182.2 2.5 reduce_sum.42
  184.7 5.5 %reduce_sum.43 = f32[128,2304]{1,0:T(8,128)} reduce(f32[128,2,2304]{2,1,0:T(2,128)} %reduce_sum.42, f32[]{:T(128)} %constant.104.clone.1), dimensions={1}, to_apply=%region_5.6 | reduce | flops 294912 | bytes 3538948 | tf_op jit(solution)/shard_map/reduce_sum | solution.py:70
  190.3 60.1 %all-reduce.4.cloned.1.call-done = f32[128,2304]{1,0:T(8,128)} async-done(((f32[128,2304]{1,0:T(8,128)}), f32[128,2304]{1,0:T(8,128)}) %all-reduce.4.cloned.1.call-update) | async-done | bytes 1179664 | tf_op jit(solution)/shard_map/psum | solution.py:73
  250.4 1.5 multiply_reduce_fusion
  252.0 1.5 multiply_convert_fusion
  253.5 6.2 %gather_fusion = bf16[1024,2304]{1,0:T(8,128)(2,1)} fusion(bf16[129,2304]{1,0:T(8,128)(2,1)S(1)} %concatenate.10, s32[1024]{0:T(1024)S(1)} %broadcast_clamp_fusion), kind=kCustom, calls=%fused_computation | custom fusion | bytes 9441280 | tf_op jit(solution)/shard_map/jit(_take)/gather | solution.py:75
  259.7 2.8 broadcast_select_fusion
  262.5 2.6 copy.96
  265.1 5.8 %all-to-all-start.2 = ((bf16[2,16,2,16,2304]{4,3,2,0,1:T(8,128)(2,1)}), bf16[2,16,2,16,2304]{4,3,2,0,1:T(8,128)(2,1)}, u32[]{:S(2)}, u32[]{:S(2)}) async-start(bf16[2,16,2,16,2304]{4,3,2,0,1:T(8,128)(2,1)} %copy.96), calls=%async_computation.2 | async-start | bytes 9437184 | tf_op jit(solution)/shard_map/all_to_all | solution.py:78
  270.9 6.9 %gather_fusion.1 = s32[1024]{0:T(1024)S(1)} fusion(s32[129]{0:T(256)S(1)} %pad_add_fusion, s32[1024]{0:T(1024)S(1)} %broadcast_clamp_fusion), kind=kCustom, calls=%fused_computation.1 | custom fusion | bytes 12288 | tf_op jit(solution)/shard_map/jit(_take)/gather | solution.py:56
  278.6 79.0 %all-to-all-done.2 = bf16[2,16,2,16,2304]{4,3,2,0,1:T(8,128)(2,1)} async-done(((bf16[2,16,2,16,2304]{4,3,2,0,1:T(8,128)(2,1)}), bf16[2,16,2,16,2304]{4,3,2,0,1:T(8,128)(2,1)}, u32[]{:S(2)}, u32[]{:S(2)}) %all-to-all-start.2) | async-done | bytes 4718624 | tf_op jit(solution)/shard_map/all_to_all | solution.py:78
  357.6 21.7 %all-to-all-start.4 = ((s32[2,16,2,16]{3,2,0,1:T(2,128)}), s32[2,16,2,16]{3,2,0,1:T(2,128)S(1)}, u32[]{:S(2)}, u32[]{:S(2)}) async-start(s32[2,16,2,16]{3,2,0,1:T(2,128)} %copy.101), calls=%async_computation.4 | async-start | bytes 65536 | tf_op jit(solution)/shard_map/all_to_all | solution.py:61
  379.4 5.2 %fusion.6 = bf16[2,16,2,16,256]{4,3,1,2,0:T(8,128)(2,1)S(1)} fusion(bf16[2,2,256,2304,1]{3,2,4,1,0:T(8,128)(2,1)} %bitcast.79, bf16[2,16,2,16,2304]{4,3,2,0,1:T(8,128)(2,1)} %all-to-all-done.2), kind=kOutput, calls=%fused_computation.13 | convolution fusion | flops 1208221696 | bytes 9961472 | tf_op jit(solution)/shard_map/lspcd,lpjd->lspcj/dot_general | solution.py:79
  384.6 0.9 copy.98
  386.0 5.5 %all-to-all-start.3 = ((bf16[2,16,2,16,256]{4,3,2,0,1:T(8,128)(2,1)}), bf16[2,16,2,16,256]{4,3,2,0,1:T(8,128)(2,1)S(1)}, u32[]{:S(2)}, u32[]{:S(2)}) async-start(bf16[2,16,2,16,256]{4,3,2,0,1:T(8,128)(2,1)} %copy.98), calls=%async_computation.3 | async-start | bytes 1048576 | tf_op jit(solution)/shard_map/all_to_all | solution.py:82
  391.9 0.7 convolution_bitcast_fusion
  392.6 0.7 reshape.203
  393.3 12.4 %all-to-all-done.3 = bf16[2,16,2,16,256]{4,3,2,0,1:T(8,128)(2,1)S(1)} async-done(((bf16[2,16,2,16,256]{4,3,2,0,1:T(8,128)(2,1)}), bf16[2,16,2,16,256]{4,3,2,0,1:T(8,128)(2,1)S(1)}, u32[]{:S(2)}, u32[]{:S(2)}) %all-to-all-start.3) | async-done | bytes 524320 | tf_op jit(solution)/shard_map/all_to_all | solution.py:82
  405.8 3.2 gather_fusion.4
  409.1 1.4 multiply_convert_fusion.1
  (60 shorter events, 5.4 us)
Async XLA Ops:
  7.2 28.4 %copy-start.5 = (s32[128]{0:T(128)S(1)}, s32[128]{0:T(128)}, u32[]{:S(2)}) copy-start(s32[128]{0:T(128)} %param.8) | copy-start | bytes 1540
  7.2 28.5 %copy-start.1 = (bf16[2,128,2,256]{3,2,1,0:T(2,128)(2,1)S(1)}, bf16[2,128,2,256]{3,2,1,0:T(2,128)(2,1)}, u32[]{:S(2)}) copy-start(bf16[2,128,2,256]{3,2,1,0:T(2,128)(2,1)} %param.6) | copy-start | bytes 786436
  70.3 91.2 %all-to-all-start.1 = ((bf16[2,16,2,16,2304]{4,3,2,0,1:T(8,128)(2,1)}), bf16[2,16,2,16,2304]{4,3,2,0,1:T(8,128)(2,1)}, u32[]{:S(2)}, u32[]{:S(2)}) async-start(bf16[2,16,2,16,2304]{4,3,2,0,1:T(8,128)(2,1)} %copy.93), calls=%async_computation.1 | async-start | bytes 9437184 | tf_op jit(solution)/shard_map/all_to_all | solution.py:66
  74.9 175.5 %all-reduce.4.cloned.1.call-start = ((), (), s32[]{:S(2)}) async-start(), calls=%async_computation.5 | async-start | bytes 2359296 | tf_op jit(solution)/shard_map/psum | solution.py:73
  182.2 68.2 %copy-start = (bf16[128,2304]{1,0:T(8,128)(2,1)S(1)}, bf16[128,2304]{1,0:T(8,128)(2,1)}, u32[]{:S(2)}) copy-start(bf16[128,2304]{1,0:T(8,128)(2,1)} %param.10) | copy-start | bytes 1769476
  265.1 5.8 %copy-start.4 = (s32[128]{0:T(128)S(1)}, s32[128]{0:T(128)}, u32[]{:S(2)}) copy-start(s32[128]{0:T(128)} %param.9) | copy-start | bytes 1540
  265.1 92.5 %all-to-all-start.2 = ((bf16[2,16,2,16,2304]{4,3,2,0,1:T(8,128)(2,1)}), bf16[2,16,2,16,2304]{4,3,2,0,1:T(8,128)(2,1)}, u32[]{:S(2)}, u32[]{:S(2)}) async-start(bf16[2,16,2,16,2304]{4,3,2,0,1:T(8,128)(2,1)} %copy.96), calls=%async_computation.2 | async-start | bytes 9437184 | tf_op jit(solution)/shard_map/all_to_all | solution.py:78
  357.6 28.4 %all-to-all-start.4 = ((s32[2,16,2,16]{3,2,0,1:T(2,128)}), s32[2,16,2,16]{3,2,0,1:T(2,128)S(1)}, u32[]{:S(2)}, u32[]{:S(2)}) async-start(s32[2,16,2,16]{3,2,0,1:T(2,128)} %copy.101), calls=%async_computation.4 | async-start | bytes 65536 | tf_op jit(solution)/shard_map/all_to_all | solution.py:61
  379.3 12.3 %copy-start.3 = (s32[2,128,2]{1,2,0:T(2,128)S(1)}, s32[2,128,2]{1,2,0:T(2,128)}, u32[]{:S(2)}) copy-start(s32[2,128,2]{1,2,0:T(2,128)} %param.7) | copy-start | bytes 6148
  384.6 24.5 %copy-start.2 = (bf16[2,128,2,256]{3,2,1,0:T(2,128)(2,1)S(1)}, bf16[2,128,2,256]{3,2,1,0:T(2,128)(2,1)}, u32[]{:S(2)}) copy-start(bf16[2,128,2,256]{3,2,1,0:T(2,128)(2,1)} %param.6) | copy-start | bytes 786436
  386.0 19.7 %all-to-all-start.3 = ((bf16[2,16,2,16,256]{4,3,2,0,1:T(8,128)(2,1)}), bf16[2,16,2,16,256]{4,3,2,0,1:T(8,128)(2,1)S(1)}, u32[]{:S(2)}, u32[]{:S(2)}) async-start(bf16[2,16,2,16,256]{4,3,2,0,1:T(8,128)(2,1)} %copy.98), calls=%async_computation.3 | async-start | bytes 1048576 | tf_op jit(solution)/shard_map/all_to_all | solution.py:82
Sparse Core Ops, SparseCore 0:
  190.3 60.0 all-reduce.3
where the time goes:
time: 418 us; the launch traced here: 417 us
  waiting for transfers between devices  238 us (57%)
  local copies, waits for them, and re-layouts  77.8 us (19%)
  starting transfers between devices  37.8 us (9%)
  blocking collectives  21.5 us (5%)
  other arithmetic  17.8 us (4%)
  between operations  14.4 us (3%)
  matrix products  9.61 us (2%)
    all_to_all x1, waiting for transfers between devices, per_device(): lax.all_to_all(built, 'tok', split_axis=1, concat_axis=1, tiled=True)  86.4 us
    all_to_all x1, waiting for transfers between devices, per_device(): lax.all_to_all(send_grad, 'tok', split_axis=1, concat_axis=1, tiled=True)  79 us
    psum x1, waiting for transfers between devices, per_device(): rebuilt = lax.psum(partial_value, 'lyr')  60.1 us
    scatter x1, local copies, waits for them, and re-layouts, source_of(): return empty.at[slot_ids].set(jnp.arange(row_count, dtype=jnp.int32))  24.5 us
    gather x4, local copies, waits for them, and re-layouts, take_rows(): return jnp.take(table, index, axis=0)  22.2 us
    all_to_all x1, starting transfers between devices, per_device(): lax.all_to_all(slot_requests, 'tok', split_axis=1, concat_axis=1, tiled=T...  21.7 us
    all_to_all x1, blocking collectives, per_device(): lax.all_to_all(send_codes, 'tok', split_axis=1, concat_axis=1, tiled=True)  21.5 us
    all_to_all x1, waiting for transfers between devices, per_device(): lax.all_to_all(projected_slots, 'tok', split_axis=1, concat_axis=1, tiled...  12.4 us
  transfers between devices with their start and end apart: 5, of which 5 were waited for; matrix products, arithmetic and copies ran while one was open for 4% of the time, Pallas kernels for 0%

commit v1 on v0

--- a/solution.py
+++ b/solution.py
@@ -6,6 +6,22 @@
 PANELS = 32
 REQUESTS = 16
 CAP = 16
+
+
+def swapped_with_each(x, axis, split, join):
+    ways, here = (lax.axis_size(axis), lax.axis_index(axis))
+    width = x.shape[split] // ways
+    lengths = list(x.shape)
+    lengths[split] = width
+    height = lengths[join]
+    lengths[join] = height * ways
+    full = jnp.zeros(lengths, x.dtype)
+    for mask in range(ways):
+        part = lax.dynamic_slice_in_dim(x, (here ^ mask) * width, width, axis=split)
+        if mask:
+            part = lax.ppermute(part, axis, [(d, d ^ mask) for d in range(ways)])
+        full = lax.dynamic_update_slice_in_dim(full, part, (here ^ mask) * height, axis=join)
+    return full
 
 
 def slot_of(flat_ids):
@@ -63,9 +79,7 @@
     built = jnp.einsum(
         "lspcj,lpjd->lspcd", received, panel_weights, preferred_element_type=jnp.float32
     ).astype(jnp.bfloat16)
-    returned = lax.all_to_all(built, "tok", split_axis=1, concat_axis=1, tiled=True).reshape(
-        layers_here, PANELS * CAP, width
-    )
+    returned = swapped_with_each(built, "tok", 1, 1).reshape(layers_here, PANELS * CAP, width)
     per_row = jax.vmap(take_rows)(returned, slot_ids)
     partial_value = jnp.sum(
         per_row.astype(jnp.float32).reshape(layers_here, count, kact, width), axis=(0, 2)

time: 418 us -> 424 us (1.014)
  starting transfers between devices: 37.8 us -> 82.8 us
  waiting for transfers between devices: 238 us -> 212 us
  blocking collectives: 21.5 us -> 0 us
  local copies, waits for them, and re-layouts: 77.8 us -> 85.9 us
    all_to_all x1, waiting for transfers between devices: 86.4 us -> 13.9 us  [per_device(): lax.all_to_all(send_codes, 'tok', split_axis=1, concat_axis=1, tiled=True)]
    ppermute x0 -> x15, waiting for transfers between devices: none -> 42.7 us  [swapped_with_each(): part = lax.ppermute(part, axis, [(d, d ^ mask) for d in range(ways)])]
    ppermute x0 -> x15, starting transfers between devices: none -> 42.2 us  [swapped_with_each(): part = lax.ppermute(part, axis, [(d, d ^ mask) for d in range(ways)])]
    all_to_all x1 -> x0, blocking collectives: 21.5 us -> none  [per_device(): lax.all_to_all(send_codes, 'tok', split_axis=1, concat_axis=1, tiled=True)]
    dynamic_update_slice x0 -> x16, local copies, waits for them, and re-layouts: none -> 11.8 us  [swapped_with_each(): lax.dynamic_update_slice_in_dim(full, part, (here ^ mask) * height, axis=...]
    all_to_all x1 -> x0, local copies, waits for them, and re-layouts: 4.86 us -> none  [per_device(): lax.all_to_all(built, 'tok', split_axis=1, concat_axis=1, tiled=True)]
  transfers between devices with their start and end apart: 5 -> 20, of which waited for: 5 -> 11; matrix products, arithmetic and copies ran while one was open for 4% -> 7% of each run, Pallas kernels for 0% -> 0%
where the time goes in v1:
time: 424 us; the launch traced here: 423 us
  waiting for transfers between devices  212 us (50%)
  local copies, waits for them, and re-layouts  85.9 us (20%)
  starting transfers between devices  82.8 us (20%)
  other arithmetic  17.8 us (4%)
  between operations  14.6 us (3%)
  matrix products  9.62 us (2%)
    all_to_all x1, waiting for transfers between devices, per_device(): lax.all_to_all(send_grad, 'tok', split_axis=1, concat_axis=1, tiled=True)  79 us
    psum x1, waiting for transfers between devices, per_device(): rebuilt = lax.psum(partial_value, 'lyr')  63.5 us
    ppermute x15, waiting for transfers between devices, swapped_with_each(): part = lax.ppermute(part, axis, [(d, d ^ mask) for d in range(ways)])  42.7 us
    ppermute x15, starting transfers between devices, swapped_with_each(): part = lax.ppermute(part, axis, [(d, d ^ mask) for d in range(ways)])  42.2 us
    scatter x1, local copies, waits for them, and re-layouts, source_of(): return empty.at[slot_ids].set(jnp.arange(row_count, dtype=jnp.int32))  24.5 us
    gather x4, local copies, waits for them, and re-layouts, take_rows(): return jnp.take(table, index, axis=0)  22.3 us
    all_to_all x1, starting transfers between devices, per_device(): lax.all_to_all(slot_requests, 'tok', split_axis=1, concat_axis=1, tiled=T...  21.7 us
    all_to_all x1, waiting for transfers between devices, per_device(): lax.all_to_all(send_codes, 'tok', split_axis=1, concat_axis=1, tiled=True)  13.9 us
  transfers between devices with their start and end apart: 20, of which 11 were waited for; matrix products, arithmetic and copies ran while one was open for 7% of the time, Pallas kernels for 0%

profile of v1, /device:TPU:0, one launch (start us, length us, event | category | flops | bytes accessed | tf_op | source)
XLA Modules:
  0.0 422.8 jit_solution(6471399462986205689)
XLA Ops:
  10.9 24.5 %scatter_fusion = s32[2,512]{1,0:T(2,128)S(1)} fusion(s32[2,512]{1,0:T(2,128)S(1)} %broadcast_in_dim.74, s32[512]{0:T(512)S(1)} %bitcast.103, s32[512]{0:T(512)S(1)} %bitcast.113), kind=kCustom, calls=%fused_computation.5 | custom fusion | bytes 10240 | tf_op jit(solution)/shard_map/vmap()/scatter | solution.py:36
  36.7 5.5 %gather_fusion.2 = bf16[1024,256]{1,0:T(8,128)(2,1)S(1)} fusion(bf16[2,257,256]{2,0,1:T(2,128)(2,1)S(1)} %concatenate.9, s32[1024]{0:T(1024)S(1)} %bitcast.102), kind=kCustom, calls=%fused_computation.2 | custom fusion | bytes 1056768 | tf_op jit(solution)/shard_map/vmap(jit(_take))/gather | solution.py:40
  43.2 7.4 %all-to-all-start = ((bf16[2,16,2,16,256]{4,3,2,0,1:T(8,128)(2,1)}), bf16[2,16,2,16,256]{4,3,2,0,1:T(8,128)(2,1)S(1)}, u32[]{:S(2)}, u32[]{:S(2)}) async-start(bf16[2,16,2,16,256]{4,3,2,0,1:T(8,128)(2,1)} %copy.84), calls=%async_computation | async-start | bytes 1048576 | tf_op jit(solution)/shard_map/all_to_all | solution.py:76
  51.0 13.9 %all-to-all-done = bf16[2,16,2,16,256]{4,3,2,0,1:T(8,128)(2,1)S(1)} async-done(((bf16[2,16,2,16,256]{4,3,2,0,1:T(8,128)(2,1)}), bf16[2,16,2,16,256]{4,3,2,0,1:T(8,128)(2,1)S(1)}, u32[]{:S(2)}, u32[]{:S(2)}) %all-to-all-start) | async-done | bytes 524320 | tf_op jit(solution)/shard_map/all_to_all | solution.py:76
  64.9 3.7 convolution_convert_fusion
  72.8 2.7 broadcast_in_dim.79
  76.2 2.1 collective-permute-start.5
  80.3 4.0 collective-permute-done.2
  84.2 2.5 collective-permute-start.7
  88.8 2.1 collective-permute-start.9
  91.6 14.1 %collective-permute-done.5 = bf16[2,1,2,16,2304]{4,3,2,1,0:T(8,128)(2,1)S(1)} collective-permute-done((bf16[2,1,2,16,2304]{4,3,2,1,0:T(8,128)(2,1)S(1)}, bf16[2,1,2,16,2304]{4,3,2,1,0:T(8,128)(2,1)S(1)}, u32[]{:S(2)}, u32[]{:S(2)}) %collective-permute-start.5) | collective-permute-done | bytes 294944 | tf_op jit(solution)/shard_map/ppermute | solution.py:22
  106.5 5.0 %collective-permute-done.6 = bf16[2,1,2,16,2304]{4,3,2,1,0:T(8,128)(2,1)S(1)} collective-permute-done((bf16[2,1,2,16,2304]{4,3,2,1,0:T(8,128)(2,1)S(1)}, bf16[2,1,2,16,2304]{4,3,2,1,0:T(8,128)(2,1)S(1)}, u32[]{:S(2)}, u32[]{:S(2)}) %collective-permute-start.6) | collective-permute-done | bytes 294944 | tf_op jit(solution)/shard_map/ppermute | solution.py:22
  111.5 2.5 collective-permute-start.11
  116.3 25.6 %collective-permute-start.13 = (bf16[2,1,2,16,2304]{4,3,2,1,0:T(8,128)(2,1)S(1)}, bf16[2,1,2,16,2304]{4,3,2,1,0:T(8,128)(2,1)S(1)}, u32[]{:S(2)}, u32[]{:S(2)}) collective-permute-start(bf16[2,1,2,16,2304]{4,3,2,1,0:T(8,128)(2,1)S(1)} %get-tuple-element.15), channel_id=1, source_target_pairs={{0,28},{2,30},{4,24},{6,26},{8,20},{10,22},{12,16},{14,18},{16,12}... | collective-permute-start | bytes 884744 | tf_op jit(solution)/shard_map/ppermute | solution.py:22
  142.6 9.5 %collective-permute-done.9 = bf16[2,1,2,16,2304]{4,3,2,1,0:T(8,128)(2,1)S(1)} collective-permute-done((bf16[2,1,2,16,2304]{4,3,2,1,0:T(8,128)(2,1)S(1)}, bf16[2,1,2,16,2304]{4,3,2,1,0:T(8,128)(2,1)S(1)}, u32[]{:S(2)}, u32[]{:S(2)}) %collective-permute-start.9) | collective-permute-done | bytes 294944 | tf_op jit(solution)/shard_map/ppermute | solution.py:22
  154.8 10.0 %collective-permute-done.10 = bf16[2,1,2,16,2304]{4,3,2,1,0:T(8,128)(2,1)S(1)} collective-permute-done((bf16[2,1,2,16,2304]{4,3,2,1,0:T(8,128)(2,1)S(1)}, bf16[2,1,2,16,2304]{4,3,2,1,0:T(8,128)(2,1)S(1)}, u32[]{:S(2)}, u32[]{:S(2)}) %collective-permute-start.10) | collective-permute-done | bytes 294944 | tf_op jit(solution)/shard_map/ppermute | solution.py:22
  168.5 13.5 %gather_fusion.3 = bf16[512,2304]{1,0:T(8,128)(2,1)} fusion(bf16[2,512,2304]{2,1,0:T(8,128)(2,1)} %bitcast.24, s32[512]{0:T(512)S(1)} %bitcast.100), kind=kCustom, calls=%fused_computation.3 | custom fusion | bytes 4722688 | tf_op jit(solution)/shard_map/vmap(jit(_take))/gather | solution.py:40
  182.0 2.4 convert_reduce_fusion
  184.3 2.5 reduce_sum.42
  186.8 5.5 %reduce_sum.43 = f32[128,2304]{1,0:T(8,128)} reduce(f32[128,2,2304]{2,1,0:T(2,128)} %reduce_sum.42, f32[]{:T(128)} %constant.137.clone.1), dimensions={1}, to_apply=%region_5.6 | reduce | flops 294912 | bytes 3538948 | tf_op jit(solution)/shard_map/reduce_sum | solution.py:84
  192.4 63.5 %all-reduce.4.cloned.1.call-done = f32[128,2304]{1,0:T(8,128)} async-done(((f32[128,2304]{1,0:T(8,128)}), f32[128,2304]{1,0:T(8,128)}) %all-reduce.4.cloned.1.call-update) | async-done | bytes 1179664 | tf_op jit(solution)/shard_map/psum | solution.py:87
  259.0 6.2 %gather_fusion = bf16[1024,2304]{1,0:T(8,128)(2,1)} fusion(bf16[129,2304]{1,0:T(8,128)(2,1)S(1)} %concatenate.10, s32[1024]{0:T(1024)S(1)} %broadcast_clamp_fusion), kind=kCustom, calls=%fused_computation | custom fusion | bytes 9441280 | tf_op jit(solution)/shard_map/jit(_take)/gather | solution.py:89
  265.2 2.8 broadcast_select_fusion
  268.1 2.6 copy.87
  270.7 5.8 %all-to-all-start.1 = ((bf16[2,16,2,16,2304]{4,3,2,0,1:T(8,128)(2,1)}), bf16[2,16,2,16,2304]{4,3,2,0,1:T(8,128)(2,1)}, u32[]{:S(2)}, u32[]{:S(2)}) async-start(bf16[2,16,2,16,2304]{4,3,2,0,1:T(8,128)(2,1)} %copy.87), calls=%async_computation.1 | async-start | bytes 9437184 | tf_op jit(solution)/shard_map/all_to_all | solution.py:92
  276.5 6.9 %gather_fusion.1 = s32[1024]{0:T(1024)S(1)} fusion(s32[129]{0:T(256)S(1)} %pad_add_fusion, s32[1024]{0:T(1024)S(1)} %broadcast_clamp_fusion), kind=kCustom, calls=%fused_computation.1 | custom fusion | bytes 12288 | tf_op jit(solution)/shard_map/jit(_take)/gather | solution.py:72
  284.1 79.0 %all-to-all-done.1 = bf16[2,16,2,16,2304]{4,3,2,0,1:T(8,128)(2,1)} async-done(((bf16[2,16,2,16,2304]{4,3,2,0,1:T(8,128)(2,1)}), bf16[2,16,2,16,2304]{4,3,2,0,1:T(8,128)(2,1)}, u32[]{:S(2)}, u32[]{:S(2)}) %all-to-all-start.1) | async-done | bytes 4718624 | tf_op jit(solution)/shard_map/all_to_all | solution.py:92
  363.1 21.7 %all-to-all-start.3 = ((s32[2,16,2,16]{3,2,0,1:T(2,128)}), s32[2,16,2,16]{3,2,0,1:T(2,128)S(1)}, u32[]{:S(2)}, u32[]{:S(2)}) async-start(s32[2,16,2,16]{3,2,0,1:T(2,128)} %copy.92), calls=%async_computation.3 | async-start | bytes 65536 | tf_op jit(solution)/shard_map/all_to_all | solution.py:77
  384.9 5.2 %fusion.5 = bf16[2,16,2,16,256]{4,3,1,2,0:T(8,128)(2,1)S(1)} fusion(bf16[2,2,256,2304,1]{3,2,4,1,0:T(8,128)(2,1)} %bitcast.108, bf16[2,16,2,16,2304]{4,3,2,0,1:T(8,128)(2,1)} %all-to-all-done.1), kind=kOutput, calls=%fused_computation.12 | convolution fusion | flops 1208221696 | bytes 9961472 | tf_op jit(solution)/shard_map/lspcd,lpjd->lspcj/dot_general | solution.py:93
  391.5 5.5 %all-to-all-start.2 = ((bf16[2,16,2,16,256]{4,3,2,0,1:T(8,128)(2,1)}), bf16[2,16,2,16,256]{4,3,2,0,1:T(8,128)(2,1)S(1)}, u32[]{:S(2)}, u32[]{:S(2)}) async-start(bf16[2,16,2,16,256]{4,3,2,0,1:T(8,128)(2,1)} %copy.89), calls=%async_computation.2 | async-start | bytes 1048576 | tf_op jit(solution)/shard_map/all_to_all | solution.py:96
  398.9 12.4 %all-to-all-done.2 = bf16[2,16,2,16,256]{4,3,2,0,1:T(8,128)(2,1)S(1)} async-done(((bf16[2,16,2,16,256]{4,3,2,0,1:T(8,128)(2,1)}), bf16[2,16,2,16,256]{4,3,2,0,1:T(8,128)(2,1)S(1)}, u32[]{:S(2)}, u32[]{:S(2)}) %all-to-all-start.2) | async-done | bytes 524320 | tf_op jit(solution)/shard_map/all_to_all | solution.py:96
  411.3 3.2 gather_fusion.4
  (105 shorter events, 34.6 us)
Async XLA Ops:
  7.2 28.4 %copy-start.5 = (s32[128]{0:T(128)S(1)}, s32[128]{0:T(128)}, u32[]{:S(2)}) copy-start(s32[128]{0:T(128)} %param.8) | copy-start | bytes 1540
  7.2 28.4 %copy-start.1 = (bf16[2,128,2,256]{3,2,1,0:T(2,128)(2,1)S(1)}, bf16[2,128,2,256]{3,2,1,0:T(2,128)(2,1)}, u32[]{:S(2)}) copy-start(bf16[2,128,2,256]{3,2,1,0:T(2,128)(2,1)} %param.6) | copy-start | bytes 786436
  43.2 21.7 %all-to-all-start = ((bf16[2,16,2,16,256]{4,3,2,0,1:T(8,128)(2,1)}), bf16[2,16,2,16,256]{4,3,2,0,1:T(8,128)(2,1)S(1)}, u32[]{:S(2)}, u32[]{:S(2)}) async-start(bf16[2,16,2,16,256]{4,3,2,0,1:T(8,128)(2,1)} %copy.84), calls=%async_computation | async-start | bytes 1048576 | tf_op jit(solution)/shard_map/all_to_all | solution.py:76
  50.6 205.3 %all-reduce.4.cloned.1.call-start = ((), (), s32[]{:S(2)}) async-start(), calls=%async_computation.4 | async-start | bytes 2359296 | tf_op jit(solution)/shard_map/psum | solution.py:87
  69.0 7.1 %collective-permute-start = (bf16[2,1,2,16,2304]{4,3,2,1,0:T(8,128)(2,1)S(1)}, bf16[2,1,2,16,2304]{4,3,2,1,0:T(8,128)(2,1)S(1)}, u32[]{:S(2)}, u32[]{:S(2)}) collective-permute-start(bf16[2,1,2,16,2304]{4,3,2,1,0:T(8,128)(2,1)S(1)} %get-tuple-element.28), channel_id=1, source_target_pairs={{0,2},{2,0},{4,6},{6,4},{8,10},{10,8},{12,14},{14,12},{16,18},{18,... | collective-permute-start | bytes 884744 | tf_op jit(solution)/shard_map/ppermute | solution.py:22
  69.3 9.9 %collective-permute-start.1 = (bf16[2,1,2,16,2304]{4,3,2,1,0:T(8,128)(2,1)S(1)}, bf16[2,1,2,16,2304]{4,3,2,1,0:T(8,128)(2,1)S(1)}, u32[]{:S(2)}, u32[]{:S(2)}) collective-permute-start(bf16[2,1,2,16,2304]{4,3,2,1,0:T(8,128)(2,1)S(1)} %get-tuple-element.27), channel_id=1, source_target_pairs={{0,4},{2,6},{4,0},{6,2},{8,12},{10,14},{12,8},{14,10},{16,20},{18,... | collective-permute-start | bytes 884744 | tf_op jit(solution)/shard_map/ppermute | solution.py:22
  70.5 13.7 %collective-permute-start.2 = (bf16[2,1,2,16,2304]{4,3,2,1,0:T(8,128)(2,1)S(1)}, bf16[2,1,2,16,2304]{4,3,2,1,0:T(8,128)(2,1)S(1)}, u32[]{:S(2)}, u32[]{:S(2)}) collective-permute-start(bf16[2,1,2,16,2304]{4,3,2,1,0:T(8,128)(2,1)S(1)} %get-tuple-element.26), channel_id=1, source_target_pairs={{0,6},{2,4},{4,2},{6,0},{8,14},{10,12},{12,10},{14,8},{16,22},{18,... | collective-permute-start | bytes 884744 | tf_op jit(solution)/shard_map/ppermute | solution.py:22
  71.0 16.5 %collective-permute-start.3 = (bf16[2,1,2,16,2304]{4,3,2,1,0:T(8,128)(2,1)S(1)}, bf16[2,1,2,16,2304]{4,3,2,1,0:T(8,128)(2,1)S(1)}, u32[]{:S(2)}, u32[]{:S(2)}) collective-permute-start(bf16[2,1,2,16,2304]{4,3,2,1,0:T(8,128)(2,1)S(1)} %get-tuple-element.25), channel_id=1, source_target_pairs={{0,8},{2,10},{4,12},{6,14},{8,0},{10,2},{12,4},{14,6},{16,24},{18,... | collective-permute-start | bytes 884744 | tf_op jit(solution)/shard_map/ppermute | solution.py:22
  72.4 16.3 %collective-permute-start.4 = (bf16[2,1,2,16,2304]{4,3,2,1,0:T(8,128)(2,1)S(1)}, bf16[2,1,2,16,2304]{4,3,2,1,0:T(8,128)(2,1)S(1)}, u32[]{:S(2)}, u32[]{:S(2)}) collective-permute-start(bf16[2,1,2,16,2304]{4,3,2,1,0:T(8,128)(2,1)S(1)} %get-tuple-element.24), channel_id=1, source_target_pairs={{0,10},{2,8},{4,14},{6,12},{8,2},{10,0},{12,6},{14,4},{16,26},{18,... | collective-permute-start | bytes 884744 | tf_op jit(solution)/shard_map/ppermute | solution.py:22
  76.2 29.5 %collective-permute-start.5 = (bf16[2,1,2,16,2304]{4,3,2,1,0:T(8,128)(2,1)S(1)}, bf16[2,1,2,16,2304]{4,3,2,1,0:T(8,128)(2,1)S(1)}, u32[]{:S(2)}, u32[]{:S(2)}) collective-permute-start(bf16[2,1,2,16,2304]{4,3,2,1,0:T(8,128)(2,1)S(1)} %get-tuple-element.23), channel_id=1, source_target_pairs={{0,12},{2,14},{4,8},{6,10},{8,4},{10,6},{12,0},{14,2},{16,28},{18,... | collective-permute-start | bytes 884744 | tf_op jit(solution)/shard_map/ppermute | solution.py:22
  79.1 32.4 %collective-permute-start.6 = (bf16[2,1,2,16,2304]{4,3,2,1,0:T(8,128)(2,1)S(1)}, bf16[2,1,2,16,2304]{4,3,2,1,0:T(8,128)(2,1)S(1)}, u32[]{:S(2)}, u32[]{:S(2)}) collective-permute-start(bf16[2,1,2,16,2304]{4,3,2,1,0:T(8,128)(2,1)S(1)} %get-tuple-element.22), channel_id=1, source_target_pairs={{0,14},{2,12},{4,10},{6,8},{8,6},{10,4},{12,2},{14,0},{16,30},{18,... | collective-permute-start | bytes 884744 | tf_op jit(solution)/shard_map/ppermute | solution.py:22
  84.2 30.5 %collective-permute-start.7 = (bf16[2,1,2,16,2304]{4,3,2,1,0:T(8,128)(2,1)S(1)}, bf16[2,1,2,16,2304]{4,3,2,1,0:T(8,128)(2,1)S(1)}, u32[]{:S(2)}, u32[]{:S(2)}) collective-permute-start(bf16[2,1,2,16,2304]{4,3,2,1,0:T(8,128)(2,1)S(1)} %get-tuple-element.21), channel_id=1, source_target_pairs={{0,16},{2,18},{4,20},{6,22},{8,24},{10,26},{12,28},{14,30},{16,0},... | collective-permute-start | bytes 884744 | tf_op jit(solution)/shard_map/ppermute | solution.py:22
  87.5 28.8 %collective-permute-start.8 = (bf16[2,1,2,16,2304]{4,3,2,1,0:T(8,128)(2,1)S(1)}, bf16[2,1,2,16,2304]{4,3,2,1,0:T(8,128)(2,1)S(1)}, u32[]{:S(2)}, u32[]{:S(2)}) collective-permute-start(bf16[2,1,2,16,2304]{4,3,2,1,0:T(8,128)(2,1)S(1)} %get-tuple-element.20), channel_id=1, source_target_pairs={{0,18},{2,16},{4,22},{6,20},{8,26},{10,24},{12,30},{14,28},{16,2},... | collective-permute-start | bytes 884744 | tf_op jit(solution)/shard_map/ppermute | solution.py:22
  88.8 63.3 %collective-permute-start.9 = (bf16[2,1,2,16,2304]{4,3,2,1,0:T(8,128)(2,1)S(1)}, bf16[2,1,2,16,2304]{4,3,2,1,0:T(8,128)(2,1)S(1)}, u32[]{:S(2)}, u32[]{:S(2)}) collective-permute-start(bf16[2,1,2,16,2304]{4,3,2,1,0:T(8,128)(2,1)S(1)} %get-tuple-element.19), channel_id=1, source_target_pairs={{0,20},{2,22},{4,16},{6,18},{8,28},{10,30},{12,24},{14,26},{16,4},... | collective-permute-start | bytes 884744 | tf_op jit(solution)/shard_map/ppermute | solution.py:22
  105.7 59.1 %collective-permute-start.10 = (bf16[2,1,2,16,2304]{4,3,2,1,0:T(8,128)(2,1)S(1)}, bf16[2,1,2,16,2304]{4,3,2,1,0:T(8,128)(2,1)S(1)}, u32[]{:S(2)}, u32[]{:S(2)}) collective-permute-start(bf16[2,1,2,16,2304]{4,3,2,1,0:T(8,128)(2,1)S(1)} %get-tuple-element.18), channel_id=1, source_target_pairs={{0,22},{2,20},{4,18},{6,16},{8,30},{10,28},{12,26},{14,24},{16,6},... | collective-permute-start | bytes 884744 | tf_op jit(solution)/shard_map/ppermute | solution.py:22
  111.5 54.0 %collective-permute-start.11 = (bf16[2,1,2,16,2304]{4,3,2,1,0:T(8,128)(2,1)S(1)}, bf16[2,1,2,16,2304]{4,3,2,1,0:T(8,128)(2,1)S(1)}, u32[]{:S(2)}, u32[]{:S(2)}) collective-permute-start(bf16[2,1,2,16,2304]{4,3,2,1,0:T(8,128)(2,1)S(1)} %get-tuple-element.17), channel_id=1, source_target_pairs={{0,24},{2,26},{4,28},{6,30},{8,16},{10,18},{12,20},{14,22},{16,8},... | collective-permute-start | bytes 884744 | tf_op jit(solution)/shard_map/ppermute | solution.py:22
  114.7 51.5 %collective-permute-start.12 = (bf16[2,1,2,16,2304]{4,3,2,1,0:T(8,128)(2,1)S(1)}, bf16[2,1,2,16,2304]{4,3,2,1,0:T(8,128)(2,1)S(1)}, u32[]{:S(2)}, u32[]{:S(2)}) collective-permute-start(bf16[2,1,2,16,2304]{4,3,2,1,0:T(8,128)(2,1)S(1)} %get-tuple-element.16), channel_id=1, source_target_pairs={{0,26},{2,24},{4,30},{6,28},{8,18},{10,16},{12,22},{14,20},{16,10}... | collective-permute-start | bytes 884744 | tf_op jit(solution)/shard_map/ppermute | solution.py:22
  116.3 50.7 %collective-permute-start.13 = (bf16[2,1,2,16,2304]{4,3,2,1,0:T(8,128)(2,1)S(1)}, bf16[2,1,2,16,2304]{4,3,2,1,0:T(8,128)(2,1)S(1)}, u32[]{:S(2)}, u32[]{:S(2)}) collective-permute-start(bf16[2,1,2,16,2304]{4,3,2,1,0:T(8,128)(2,1)S(1)} %get-tuple-element.15), channel_id=1, source_target_pairs={{0,28},{2,30},{4,24},{6,26},{8,20},{10,22},{12,16},{14,18},{16,12}... | collective-permute-start | bytes 884744 | tf_op jit(solution)/shard_map/ppermute | solution.py:22
  152.0 15.7 %collective-permute-start.14 = (bf16[2,1,2,16,2304]{4,3,2,1,0:T(8,128)(2,1)S(1)}, bf16[2,1,2,16,2304]{4,3,2,1,0:T(8,128)(2,1)S(1)}, u32[]{:S(2)}, u32[]{:S(2)}) collective-permute-start(bf16[2,1,2,16,2304]{4,3,2,1,0:T(8,128)(2,1)S(1)} %get-tuple-element.14), channel_id=1, source_target_pairs={{0,30},{2,28},{4,26},{6,24},{8,22},{10,20},{12,18},{14,16},{16,14}... | collective-permute-start | bytes 884744 | tf_op jit(solution)/shard_map/ppermute | solution.py:22
  184.3 71.6 %copy-start = (bf16[128,2304]{1,0:T(8,128)(2,1)S(1)}, bf16[128,2304]{1,0:T(8,128)(2,1)}, u32[]{:S(2)}) copy-start(bf16[128,2304]{1,0:T(8,128)(2,1)} %param.10) | copy-start | bytes 1769476
  270.7 5.8 %copy-start.4 = (s32[128]{0:T(128)S(1)}, s32[128]{0:T(128)}, u32[]{:S(2)}) copy-start(s32[128]{0:T(128)} %param.9) | copy-start | bytes 1540
  270.7 92.5 %all-to-all-start.1 = ((bf16[2,16,2,16,2304]{4,3,2,0,1:T(8,128)(2,1)}), bf16[2,16,2,16,2304]{4,3,2,0,1:T(8,128)(2,1)}, u32[]{:S(2)}, u32[]{:S(2)}) async-start(bf16[2,16,2,16,2304]{4,3,2,0,1:T(8,128)(2,1)} %copy.87), calls=%async_computation.1 | async-start | bytes 9437184 | tf_op jit(solution)/shard_map/all_to_all | solution.py:92
  363.1 28.4 %all-to-all-start.3 = ((s32[2,16,2,16]{3,2,0,1:T(2,128)}), s32[2,16,2,16]{3,2,0,1:T(2,128)S(1)}, u32[]{:S(2)}, u32[]{:S(2)}) async-start(s32[2,16,2,16]{3,2,0,1:T(2,128)} %copy.92), calls=%async_computation.3 | async-start | bytes 65536 | tf_op jit(solution)/shard_map/all_to_all | solution.py:77
  384.9 12.3 %copy-start.3 = (s32[2,128,2]{1,2,0:T(2,128)S(1)}, s32[2,128,2]{1,2,0:T(2,128)}, u32[]{:S(2)}) copy-start(s32[2,128,2]{1,2,0:T(2,128)} %param.7) | copy-start | bytes 6148
  390.1 24.5 %copy-start.2 = (bf16[2,128,2,256]{3,2,1,0:T(2,128)(2,1)S(1)}, bf16[2,128,2,256]{3,2,1,0:T(2,128)(2,1)}, u32[]{:S(2)}) copy-start(bf16[2,128,2,256]{3,2,1,0:T(2,128)(2,1)} %param.6) | copy-start | bytes 786436
  391.5 19.8 %all-to-all-start.2 = ((bf16[2,16,2,16,256]{4,3,2,0,1:T(8,128)(2,1)}), bf16[2,16,2,16,256]{4,3,2,0,1:T(8,128)(2,1)S(1)}, u32[]{:S(2)}, u32[]{:S(2)}) async-start(bf16[2,16,2,16,256]{4,3,2,0,1:T(8,128)(2,1)} %copy.89), calls=%async_computation.2 | async-start | bytes 1048576 | tf_op jit(solution)/shard_map/all_to_all | solution.py:96
Sparse Core Ops, SparseCore 0:
  192.4 63.4 all-reduce.3
